TPU v7x, 256 devices: a whole 4x4x8 slice. The times are simulated.
256 devices in a mesh: dp: 4 (over x), group: 4 (over y), member: 16 (over z, core).
Axes of the slice: x: 4, y: 4, z: 8, core: 2. Of those that a mesh axis runs over, the one named last changes fastest.
Arguments:
- tokens: bfloat16 [2048, 2880], P(('dp', 'group', 'member')), may hold values from -6 to 6
- cotangent: bfloat16 [2048, 2880], P(('dp', 'group', 'member')), may hold values from -6 to 6
- expert_ids: int32 [2048, 4], P(('dp', 'group', 'member')), may hold values from 0 to 7, all different within a row; in each aligned block of 8 rows (0 to 7, 8 to 15, ...) at most 8 rows name the same one
- gate_weights: float32 [2048, 4], P(('dp', 'group', 'member')), may hold values from 0.25 to 1
- w_gate: bfloat16 [8, 2880, 2880], P('group', 'member'), may hold values from -0.109375 to 0.109375
- w_up: bfloat16 [8, 2880, 2880], P('group', 'member'), may hold values from -0.109375 to 0.109375
- w_down: bfloat16 [8, 2880, 2880], P('group', 'member'), may hold values from -0.109375 to 0.109375
Outputs:
- grad_tokens: bfloat16 [2048, 2880], P(('dp', 'group', 'member'))
- grad_gate: bfloat16 [8, 2880, 2880], P('group', 'member', 'dp')
- grad_up: bfloat16 [8, 2880, 2880], P('group', 'member', 'dp')
- grad_down: bfloat16 [8, 2880, 2880], P('group', 'member', 'dp')
Inputs may be any that keep to these rules, and one draw needn't show every extreme that they name: `expert_ids`: each row names 4 different experts. Among the rows of one device no expert is named by more than 8 rows, a bound that some block reaches of them.
All inputs are finite; a program needn't handle non-finite values.
Results may differ from a plain program's by a relative error of at most 0.02.
Values may be sent and summed in bfloat16 or wider, within the bound.
No kernel may reach another device: no remote copies, remote signals or barrier semaphores. Data moves between devices by JAX's collectives and lax.ppermute only.
A program may use at most 128 MiB of HBM per device.

v0:
```python
import jax
import jax.numpy as jnp
from jax import lax
from jax.sharding import PartitionSpec as P


def on_device(tokens, cotangent, expert_ids, gate_weights, w_gate, w_up, w_down):
    n_group = lax.axis_size("group")
    n_member = lax.axis_size("member")
    local_experts = w_gate.shape[0]
    experts = local_experts * n_group
    tok_rows = tokens.shape[0]
    top_count = expert_ids.shape[1]
    model_width = tokens.shape[1]
    capacity = 2 * tok_rows * top_count // experts
    slot_block = local_experts * capacity
    flat_ids = expert_ids.reshape(-1)
    picked = (flat_ids[:, None] == jnp.arange(experts, dtype=jnp.int32)[None, :]).astype(jnp.int32)
    before = jnp.cumsum(picked, axis=0) - picked
    slot_index = jnp.sum(before * picked, axis=1)
    target = flat_ids * capacity + slot_index
    target_hot = (
        target[:, None] == jnp.arange(experts * capacity, dtype=jnp.int32)[None, :]
    ).astype(jnp.float32)
    owner_index = jnp.arange(tok_rows * top_count, dtype=jnp.int32) // top_count
    owner_hot = (owner_index[:, None] == jnp.arange(tok_rows, dtype=jnp.int32)[None, :]).astype(
        jnp.float32
    )
    placing = jnp.dot(target_hot.T, owner_hot, precision=lax.Precision.HIGHEST)
    weighted = jnp.dot(
        (target_hot * gate_weights.reshape(-1)[:, None]).T,
        owner_hot,
        precision=lax.Precision.HIGHEST,
    )
    sent_inputs = jnp.dot(
        placing.astype(jnp.bfloat16), tokens, preferred_element_type=jnp.float32
    ).astype(jnp.bfloat16)
    sent_scaled = jnp.dot(
        weighted, cotangent.astype(jnp.float32), precision=lax.Precision.HIGHEST
    ).astype(jnp.bfloat16)
    outgoing = jnp.stack([sent_inputs, sent_scaled])
    landed = lax.all_to_all(
        outgoing.reshape(2, n_group, slot_block, model_width),
        "group",
        split_axis=1,
        concat_axis=1,
        tiled=True,
    )
    arrived = lax.all_gather(
        landed.reshape(2, 1, n_group, slot_block, model_width), "member", axis=1, tiled=True
    )
    arrived_data = arrived.reshape(2, n_member * n_group, local_experts, capacity, model_width)
    inputs_rows = arrived_data[0]
    scaled_rows = arrived_data[1]
    gate_pre = jnp.einsum("rjcd,jhd->rjch", inputs_rows, w_gate, preferred_element_type=jnp.float32)
    up_pre = jnp.einsum("rjcd,jhd->rjch", inputs_rows, w_up, preferred_element_type=jnp.float32)
    sigmoid_gate = jax.nn.sigmoid(gate_pre)
    hidden = (gate_pre * sigmoid_gate * up_pre).astype(jnp.bfloat16)
    grad_hidden = jnp.einsum(
        "rjcd,jhd->rjch", scaled_rows, w_down, preferred_element_type=jnp.float32
    )
    grad_up_pre = (grad_hidden * gate_pre * sigmoid_gate).astype(jnp.bfloat16)
    grad_gate_pre = (
        grad_hidden * up_pre * sigmoid_gate * (1.0 + gate_pre * (1.0 - sigmoid_gate))
    ).astype(jnp.bfloat16)
    weight_gate = jnp.einsum(
        "rjch,rjcd->jhd", grad_gate_pre, inputs_rows, preferred_element_type=jnp.float32
    )
    weight_up = jnp.einsum(
        "rjch,rjcd->jhd", grad_up_pre, inputs_rows, preferred_element_type=jnp.float32
    )
    weight_down = jnp.einsum(
        "rjch,rjcd->jhd", hidden, scaled_rows, preferred_element_type=jnp.float32
    )
    own_rows = n_group * slot_block
    summed = jnp.einsum("rjch,jhd->rjcd", grad_gate_pre, w_gate, preferred_element_type=jnp.float32)
    summed = summed + jnp.einsum(
        "rjch,jhd->rjcd", grad_up_pre, w_up, preferred_element_type=jnp.float32
    )
    reduced = lax.psum_scatter(
        summed.reshape(lax.axis_size("member") * own_rows, model_width).astype(jnp.bfloat16),
        "member",
        scatter_dimension=0,
        tiled=True,
    )
    mine = reduced.reshape(n_group, slot_block, model_width)
    returned = lax.all_to_all(mine, "group", split_axis=0, concat_axis=0, tiled=True).reshape(
        experts * capacity, model_width
    )
    grad_tokens = jnp.dot(
        placing.T.astype(jnp.bfloat16), returned, preferred_element_type=jnp.float32
    ).astype(jnp.bfloat16)
    summed_weights = (
        lax.psum_scatter(
            weight_gate.astype(jnp.bfloat16), "dp", scatter_dimension=2, tiled=True
        ).astype(jnp.float32),
        lax.psum_scatter(
            weight_up.astype(jnp.bfloat16), "dp", scatter_dimension=2, tiled=True
        ).astype(jnp.float32),
        lax.psum_scatter(
            weight_down.astype(jnp.bfloat16), "dp", scatter_dimension=2, tiled=True
        ).astype(jnp.float32),
    )
    return (
        grad_tokens,
        summed_weights[0].astype(jnp.bfloat16),
        summed_weights[1].astype(jnp.bfloat16),
        summed_weights[2].astype(jnp.bfloat16),
    )


def solution(mesh):
    placed = (
        P(("dp", "group", "member"), None),
        P(("dp", "group", "member"), None),
        P(("dp", "group", "member"), None),
        P(("dp", "group", "member"), None),
        P("group", "member", None),
        P("group", "member", None),
        P("group", "member", None),
    )
    return jax.shard_map(
        on_device,
        mesh=mesh,
        in_specs=placed,
        out_specs=(
            P(("dp", "group", "member"), None),
            P("group", "member", "dp"),
            P("group", "member", "dp"),
            P("group", "member", "dp"),
        ),
        check_vma=False,
    )
```

profile of v0, /device:TPU:1, one launch (start us, length us, event | category | flops | bytes accessed | tf_op | source)
XLA Modules:
  0.0 319.9 jit_solution(6226053942061887606)
XLA Ops:
  7.2 0.9 copy.47
  8.1 0.1 reshape.55
  8.2 0.8 copy.48
  9.0 0.1 mul.50
  9.0 0.1 fusion.57
  9.1 0.1 reduce_window_sum.11
  9.2 0.2 select_reduce_fusion
  9.4 0.3 convolution_convert_fusion.3
  9.6 0.3 fusion.55
  9.9 1.3 convolution_convert_fusion
  11.2 1.1 convolution_convert_fusion.1
  12.3 0.1 pad_maximum_fusion
  12.4 15.9 %all_to_all.10 = bf16[2,4,16,2880]{3,2,0,1:T(8,128)(2,1)S(1)} all-to-all(bf16[2,4,16,2880]{3,2,0,1:T(8,128)(2,1)S(1)} %pad_maximum_fusion), channel_id=1, replica_groups=mesh['dp'=4,'group'=4,'member'=16] {'group'}, dimensions={1} | all-to-all | bytes 1474560 | tf_op jit(solution)/shard_map/all_to_all | solution.py:42
  28.3 0.9 copy.51
  29.2 0.0 reduce-scatter.11.cloned.1.call-start
  29.3 75.7 %all-gather.3.cloned.1.call-done = bf16[2,64,16,2880]{3,2,1,0:T(8,128)(2,1)} async-done(((bf16[2,4,16,2880]{3,2,1,0:T(8,128)(2,1)}), bf16[2,64,16,2880]{3,2,1,0:T(8,128)(2,1)}) %all-gather.3.cloned.1.call-update) | async-done | bytes 11796496 | tf_op jit(solution)/shard_map/all_gather | solution.py:49
  105.0 9.7 %slice_bitcast_fusion.1 = (bf16[64,2,8,2880]{3,2,1,0:T(8,128)(2,1)}, bf16[64,2,8,2880]{3,2,1,0:T(8,128)(2,1)}) fusion(bf16[2,64,16,2880]{3,2,1,0:T(8,128)(2,1)} %all-gather.3.cloned.1.call-done), kind=kLoop, calls=%fused_computation.2 | loop fusion | bytes 23592960 | tf_op jit(solution)/shard_map/squeeze | solution.py:54
  114.7 5.3 %fusion.47 = f32[64,2,8,180]{3,2,0,1:T(8,128)S(1)} fusion(bf16[2,180,2880,1]{2,0,1,3:T(2,128)(2,1)} %bitcast.70, bf16[64,2,8,2880]{3,2,1,0:T(8,128)(2,1)} %get-tuple-element.16), kind=kOutput, calls=%fused_computation.33 | convolution fusion | flops 1061683200 | bytes 8709120 | tf_op jit(solution)/shard_map/rjcd,jhd->rjch/dot_general | solution.py:59
  120.0 0.4 copy-done.3
  120.4 1.8 fusion.42
  122.2 3.0 multiply_convert_fusion
  125.2 1.8 fusion.32
  127.0 4.4 %fusion.12 = bf16[64,2,8,2880]{3,2,0,1:T(8,128)(2,1)} fusion(f32[2,64,8,2880]{3,2,1,0:T(8,128)S(1)} %fusion.32, bf16[64,2,8,180]{3,2,0,1:T(8,128)(2,1)S(1)} %get-tuple-element.20, bf16[2,180,2880,1]{2,0,1,3:T(2,128)(2,1)S(1)} %bitcast.56), kind=kOutput, calls=%fused_computation.15 | convolution fusion | flops 1067581440 | bytes 20136960 | tf_op jit(solution)/shard_map/rjch,jhd->rjcd/dot_general | solution.py:77
  131.4 5.7 %copy.60 = bf16[64,2,8,2880]{3,2,1,0:T(8,128)(2,1)} copy(bf16[64,2,8,2880]{3,2,0,1:T(8,128)(2,1)} %fusion.12) | data formatting | bytes 11796480 | tf_op jit(solution)/shard_map/convert_element_type | solution.py:81
  137.2 0.2 reduce-scatter.17.cloned.1.call-start
  137.4 0.8 copy-done.4
  138.2 5.5 %fusion.22 = bf16[2,180,2880]{2,1,0:T(8,128)(2,1)} fusion(bf16[64,2,8,2880]{3,2,1,0:T(8,128)(2,1)} %get-tuple-element.16, bf16[64,2,8,180]{3,2,0,1:T(8,128)(2,1)S(1)} %copy-done.4), kind=kOutput, calls=%fused_computation.19 | convolution fusion | flops 1062720000 | bytes 8340480 | tf_op jit(solution)/shard_map/rjch,rjcd->jhd/dot_general | solution.py:72
  143.7 8.4 %copy.92 = bf16[2,180,2880]{1,0,2:T(2,128)(2,1)} copy(bf16[2,180,2880]{2,1,0:T(8,128)(2,1)} %fusion.22) | data formatting | bytes 4147200
  152.2 7.4 %reshape.76 = bf16[2880,360]{1,0:T(8,128)(2,1)} reshape(bf16[2880,2,180]{2,1,0:T(2,128)(2,1)} %bitcast.58) | data formatting | bytes 4147200
  159.6 0.0 reduce-scatter.15.cloned.1.call-start
  159.7 5.6 %fusion.25 = bf16[2,180,2880]{2,1,0:T(8,128)(2,1)} fusion(bf16[64,2,8,2880]{3,2,1,0:T(8,128)(2,1)} %get-tuple-element.17, bf16[64,2,8,180]{3,2,0,1:T(8,128)(2,1)S(1)} %get-tuple-element.20), kind=kOutput, calls=%fused_computation.20 | convolution fusion | flops 1062720000 | bytes 8340480 | tf_op jit(solution)/shard_map/rjch,rjcd->jhd/dot_general | solution.py:69
  165.3 8.4 %copy.90 = bf16[2,180,2880]{1,0,2:T(2,128)(2,1)} copy(bf16[2,180,2880]{2,1,0:T(8,128)(2,1)} %fusion.25) | data formatting | bytes 4147200
  173.7 7.4 %reshape.74 = bf16[2880,360]{1,0:T(8,128)(2,1)} reshape(bf16[2880,2,180]{2,1,0:T(2,128)(2,1)} %bitcast.59) | data formatting | bytes 4147200
  181.1 0.0 reduce-scatter.13.cloned.1.call-start
  181.2 5.7 %fusion.28 = bf16[2,180,2880]{2,1,0:T(8,128)(2,1)} fusion(bf16[64,2,8,2880]{3,2,1,0:T(8,128)(2,1)} %get-tuple-element.17, bf16[64,2,8,180]{3,2,0,1:T(8,128)(2,1)S(1)} %get-tuple-element.19), kind=kOutput, calls=%fused_computation.21 | convolution fusion | flops 1062720000 | bytes 8340480 | tf_op jit(solution)/shard_map/rjch,rjcd->jhd/dot_general | solution.py:66
  186.9 8.4 %copy.88 = bf16[2,180,2880]{1,0,2:T(2,128)(2,1)} copy(bf16[2,180,2880]{2,1,0:T(8,128)(2,1)} %fusion.28) | data formatting | bytes 4147200
  195.3 7.6 %reshape.72 = bf16[2880,360]{1,0:T(8,128)(2,1)} reshape(bf16[2880,2,180]{2,1,0:T(2,128)(2,1)} %bitcast.60) | data formatting | bytes 4147200
  203.0 4.0 %all-to-all-start.1 = ((bf16[4,16,2880]{2,1,0:T(8,128)(2,1)}), bf16[4,16,2880]{2,1,0:T(8,128)(2,1)S(1)}, u32[]{:S(2)}, u32[]{:S(2)}) async-start(bf16[4,16,2880]{2,1,0:T(8,128)(2,1)} %bitcast.69), calls=%async_computation.2 | async-start | bytes 753664 | tf_op jit(solution)/shard_map/all_to_all | solution.py:87
  207.0 29.6 %reduce-scatter.17.cloned.1.call-done = bf16[720,360]{1,0:T(8,128)(2,1)} async-done(((bf16[2880,360]{1,0:T(8,128)(2,1)}), bf16[720,360]{1,0:T(8,128)(2,1)}) %reduce-scatter.17.cloned.1.call-update) | async-done | bytes 518416
  236.5 2.5 reshape.77
  239.1 2.5 copy.69
  241.6 30.4 %reduce-scatter.15.cloned.1.call-done = bf16[720,360]{1,0:T(8,128)(2,1)} async-done(((bf16[2880,360]{1,0:T(8,128)(2,1)}), bf16[720,360]{1,0:T(8,128)(2,1)}) %reduce-scatter.15.cloned.1.call-update) | async-done | bytes 518416
  272.0 2.5 reshape.75
  274.5 2.5 copy.68
  277.1 30.4 %reduce-scatter.13.cloned.1.call-done = bf16[720,360]{1,0:T(8,128)(2,1)} async-done(((bf16[2880,360]{1,0:T(8,128)(2,1)}), bf16[720,360]{1,0:T(8,128)(2,1)}) %reduce-scatter.13.cloned.1.call-update) | async-done | bytes 518416
  307.5 2.5 reshape.73
  310.0 2.5 copy.67
  312.6 0.8 convolution_convert_fusion.2
  (17 shorter events, 0.2 us)
Async XLA Ops:
  7.2 115.1 %copy-start = (bf16[2,180,2880]{2,0,1:T(2,128)(2,1)S(1)}, bf16[2,180,2880]{2,0,1:T(2,128)(2,1)}, u32[]{:S(2)}) copy-start(bf16[2,180,2880]{2,0,1:T(2,128)(2,1)} %param.12) | copy-start | bytes 6220804
  7.2 97.8 %all-gather.3.cloned.1.call-start = ((), (), s32[]{:S(2)}) async-start(), calls=%async_computation.7 | async-start | bytes 12812288 | tf_op jit(solution)/shard_map/all_gather | solution.py:49
  29.2 173.7 %reduce-scatter.11.cloned.1.call-start = ((), (), s32[]{:S(2)}) async-start(), calls=%async_computation.6 | async-start | bytes 6406144 | tf_op jit(solution)/shard_map/reduce_scatter | solution.py:80
  114.7 5.3 %copy-start.2 = (bf16[64,2,8,2880]{3,2,1,0:T(8,128)(2,1)S(1)}, bf16[64,2,8,2880]{3,2,1,0:T(8,128)(2,1)}, u32[]{:S(2)}) copy-start(bf16[64,2,8,2880]{3,2,1,0:T(8,128)(2,1)} %get-tuple-element.17) | copy-start | bytes 17694724
  114.7 5.7 %copy-start.3 = (bf16[2,180,2880]{2,0,1:T(2,128)(2,1)S(1)}, bf16[2,180,2880]{2,0,1:T(2,128)(2,1)}, u32[]{:S(2)}) copy-start(bf16[2,180,2880]{2,0,1:T(2,128)(2,1)} %param.11) | copy-start | bytes 6220804
  137.1 1.0 copy-start.4
  137.2 99.4 %reduce-scatter.17.cloned.1.call-start = ((), (), s32[]{:S(2)}) async-start(), calls=%async_computation.10 | async-start | bytes 2764800
  159.6 112.4 %reduce-scatter.15.cloned.1.call-start = ((), (), s32[]{:S(2)}) async-start(), calls=%async_computation.9 | async-start | bytes 2764800
  181.1 126.3 %reduce-scatter.13.cloned.1.call-start = ((), (), s32[]{:S(2)}) async-start(), calls=%async_computation.8 | async-start | bytes 2764800
  195.3 118.0 %copy-start.1 = (bf16[2,180,2880]{2,0,1:T(2,128)(2,1)S(1)}, bf16[2,180,2880]{2,0,1:T(2,128)(2,1)}, u32[]{:S(2)}) copy-start(bf16[2,180,2880]{2,0,1:T(2,128)(2,1)} %param.12) | copy-start | bytes 6220804
  203.0 109.6 %all-to-all-start.1 = ((bf16[4,16,2880]{2,1,0:T(8,128)(2,1)}), bf16[4,16,2880]{2,1,0:T(8,128)(2,1)S(1)}, u32[]{:S(2)}, u32[]{:S(2)}) async-start(bf16[4,16,2880]{2,1,0:T(8,128)(2,1)} %bitcast.69), calls=%async_computation.2 | async-start | bytes 753664 | tf_op jit(solution)/shard_map/all_to_all | solution.py:87
Sparse Core Ops, SparseCore 0:
  29.4 75.5 all-gather.2
  137.3 61.5 reduce-scatter.10
  201.4 35.0 reduce-scatter.16
  238.9 32.9 reduce-scatter.14
  274.4 33.0 reduce-scatter.12
where the time goes:
time: 321 us; the launch traced here: 320 us
  waiting for transfers between devices  166 us (52%)
  local copies, waits for them, and re-layouts  82.2 us (26%)
  matrix products  36.9 us (11%)
  blocking collectives  15.9 us (5%)
  between operations  13.9 us (4%)
  starting transfers between devices  4.37 us (1%)
    unnamed x8, waiting for transfers between devices  90.5 us
    all_gather x1, waiting for transfers between devices, on_device(): lax.all_gather(landed.reshape(2, 1, n_group, slot_block, model_width), 'm...  75.7 us
    unnamed x24, local copies, waits for them, and re-layouts  65.7 us
    all_to_all x1, blocking collectives, on_device(): lax.all_to_all(outgoing.reshape(2, n_group, slot_block, model_width), 'gr...  15.9 us
    squeeze x1, local copies, waits for them, and re-layouts, on_device(): scaled_rows = arrived_data[1]  9.69 us
  transfers between devices with their start and end apart: 6, of which 4 were waited for; matrix products, arithmetic and copies ran while one was open for 25% of the time, Pallas kernels for 0%

commit v1 on v0

--- a/solution.py
+++ b/solution.py
@@ -46,9 +46,11 @@
         concat_axis=1,
         tiled=True,
     )
-    arrived = lax.all_gather(
-        landed.reshape(2, 1, n_group, slot_block, model_width), "member", axis=1, tiled=True
-    )
+    own = landed.reshape(2, 1, n_group, slot_block, model_width)
+    n_dev = lax.axis_size("member")
+    shards = jnp.stack([own for _ in range(n_dev)])
+    shards = lax.all_to_all(shards, "member", split_axis=0, concat_axis=0)
+    arrived = jnp.concatenate(shards, axis=1)
     arrived_data = arrived.reshape(2, n_member * n_group, local_experts, capacity, model_width)
     inputs_rows = arrived_data[0]
     scaled_rows = arrived_data[1]

time: 321 us -> 528 us (1.64)
  blocking collectives: 15.9 us -> 291 us
  waiting for transfers between devices: 166 us -> 87.5 us
  local copies, waits for them, and re-layouts: 82.2 us -> 92.9 us
    all_to_all x0 -> x1, blocking collectives: none -> 275 us  [on_device(): shards = lax.all_to_all(shards, 'member', split_axis=0, concat_axis=0)]
    all_gather x1 -> x0, waiting for transfers between devices: 75.7 us -> none  [on_device(): lax.all_gather(landed.reshape(2, 1, n_group, slot_block, model_width), 'm...]
    slice x0 -> x1, local copies, waits for them, and re-layouts: none -> 9.72 us  [on_device(): scaled_rows = arrived_data[1]]
    squeeze x1 -> x0, local copies, waits for them, and re-layouts: 9.69 us -> none  [on_device(): scaled_rows = arrived_data[1]]
    another operation x0 -> x1, local copies, waits for them, and re-layouts: none -> 5.88 us  [on_device(): shards = jnp.stack([own for _ in range(n_dev)])]
    all_to_all x0 -> x1, local copies, waits for them, and re-layouts: none -> 5.73 us  [on_device(): shards = lax.all_to_all(shards, 'member', split_axis=0, concat_axis=0)]
    unnamed x8 -> x7, waiting for transfers between devices: 90.5 us -> 87.5 us
  transfers between devices with their start and end apart: 6 -> 5, of which waited for: 4 -> 3; matrix products, arithmetic and copies ran while one was open for 25% -> 15% of each run, Pallas kernels for 0% -> 0%
where the time goes in v1:
time: 528 us; the launch traced here: 526 us
  blocking collectives  291 us (55%)
  local copies, waits for them, and re-layouts  92.9 us (18%)
  waiting for transfers between devices  87.5 us (17%)
  matrix products  36.9 us (7%)
  between operations  13.9 us (3%)
    all_to_all x1, blocking collectives, on_device(): shards = lax.all_to_all(shards, 'member', split_axis=0, concat_axis=0)  275 us
    unnamed x7, waiting for transfers between devices  87.5 us
    unnamed x24, local copies, waits for them, and re-layouts  65.7 us
    all_to_all x1, blocking collectives, on_device(): lax.all_to_all(outgoing.reshape(2, n_group, slot_block, model_width), 'gr...  15.9 us
  transfers between devices with their start and end apart: 5, of which 3 were waited for; matrix products, arithmetic and copies ran while one was open for 15% of the time, Pallas kernels for 0%

profile of v1, /device:TPU:1, one launch (start us, length us, event | category | flops | bytes accessed | tf_op | source)
XLA Modules:
  0.0 526.2 jit_solution(15100854044420625088)
XLA Ops:
  7.2 0.9 copy.47
  8.1 0.1 reshape.56
  8.2 0.8 copy.48
  9.0 0.1 mul.50
  9.0 0.1 fusion.57
  9.1 0.1 reduce_window_sum.11
  9.2 0.2 select_reduce_fusion
  9.4 0.3 convolution_convert_fusion.3
  9.6 0.3 fusion.55
  9.9 1.3 convolution_convert_fusion
  11.2 1.1 convolution_convert_fusion.1
  12.3 0.1 pad_maximum_fusion
  12.4 15.9 %all_to_all.15 = bf16[2,4,16,2880]{3,2,0,1:T(8,128)(2,1)S(1)} all-to-all(bf16[2,4,16,2880]{3,2,0,1:T(8,128)(2,1)S(1)} %pad_maximum_fusion), channel_id=1, replica_groups=mesh['dp'=4,'group'=4,'member'=16] {'group'}, dimensions={1} | all-to-all | bytes 1474560 | tf_op jit(solution)/shard_map/all_to_all | solution.py:42
  28.3 0.1 copy.51
  28.3 5.9 %stack.15 = bf16[16,2,1,4,16,2880]{5,4,3,2,1,0:T(8,128)(2,1)} broadcast(bf16[2,4,16,2880]{3,2,1,0:T(8,128)(2,1)S(1)} %copy.51), dimensions={1,3,4,5} | broadcast | bytes 12533760 | tf_op jit(solution)/shard_map/stack | solution.py:51
  34.2 274.7 %all_to_all.16 = bf16[16,2,1,4,16,2880]{5,4,3,2,1,0:T(8,128)(2,1)S(1)} all-to-all(bf16[16,2,1,4,16,2880]{5,4,3,2,1,0:T(8,128)(2,1)} %stack.15), channel_id=1, replica_groups=mesh['dp'=4,'group'=4,'member'=16] {'member'}, dimensions={0} | all-to-all | bytes 23592960 | tf_op jit(solution)/shard_map/all_to_all | solution.py:52
  308.9 5.7 %copy.155 = bf16[16,2,1,4,16,2880]{5,4,3,0,2,1:T(8,128)(2,1)} copy(bf16[16,2,1,4,16,2880]{5,4,3,2,1,0:T(8,128)(2,1)S(1)} %all_to_all.16) | data formatting | bytes 23592960 | tf_op jit(solution)/shard_map/all_to_all | solution.py:52
  314.6 9.7 %fusion.65 = (bf16[1,16,1,4,16,2880]{5,4,3,1,2,0:T(8,128)(2,1)}, bf16[1,16,1,4,16,2880]{5,4,3,1,2,0:T(8,128)(2,1)}) fusion(bf16[2,16,1,4,16,2880]{5,4,3,1,2,0:T(8,128)(2,1)} %bitcast.58), kind=kLoop, calls=%fused_computation.61 | loop fusion | bytes 23592960 | tf_op jit(solution)/shard_map/slice | solution.py:56
  324.3 5.3 %fusion.47 = f32[64,2,8,180]{3,2,0,1:T(8,128)S(1)} fusion(bf16[2,180,2880,1]{2,0,1,3:T(2,128)(2,1)} %bitcast.78, bf16[64,2,8,2880]{3,2,1,0:T(8,128)(2,1)} %bitcast.67), kind=kOutput, calls=%fused_computation.32 | convolution fusion | flops 1061683200 | bytes 8709120 | tf_op jit(solution)/shard_map/rjcd,jhd->rjch/dot_general | solution.py:61
  329.7 0.4 copy-done.3
  330.0 1.8 fusion.42
  331.9 3.0 multiply_convert_fusion
  334.9 1.8 fusion.32
  336.7 4.4 fusion.12
  341.1 5.7 %copy.61 = bf16[64,2,8,2880]{3,2,1,0:T(8,128)(2,1)} copy(bf16[64,2,8,2880]{3,2,0,1:T(8,128)(2,1)} %fusion.12) | data formatting | bytes 11796480 | tf_op jit(solution)/shard_map/convert_element_type | solution.py:83
  346.8 0.2 reduce-scatter.17.cloned.1.call-start
  347.1 0.8 copy-done.4
  347.8 5.6 %fusion.22 = bf16[2,180,2880]{2,1,0:T(8,128)(2,1)} fusion(bf16[64,2,8,2880]{3,2,1,0:T(8,128)(2,1)} %bitcast.68, bf16[64,2,8,180]{3,2,0,1:T(8,128)(2,1)S(1)} %copy-done.4), kind=kOutput, calls=%fused_computation.18 | convolution fusion | flops 1062720000 | bytes 8340480 | tf_op jit(solution)/shard_map/rjch,rjcd->jhd/dot_general | solution.py:74
  353.4 8.4 %copy.93 = bf16[2,180,2880]{1,0,2:T(2,128)(2,1)} copy(bf16[2,180,2880]{2,1,0:T(8,128)(2,1)} %fusion.22) | data formatting | bytes 4147200
  361.8 7.4 %reshape.72 = bf16[2880,360]{1,0:T(8,128)(2,1)} reshape(bf16[2880,2,180]{2,1,0:T(2,128)(2,1)} %bitcast.60) | data formatting | bytes 4147200
  369.3 0.0 reduce-scatter.15.cloned.1.call-start
  369.3 5.6 %fusion.25 = bf16[2,180,2880]{2,1,0:T(8,128)(2,1)} fusion(bf16[64,2,8,2880]{3,2,1,0:T(8,128)(2,1)} %bitcast.63, bf16[64,2,8,180]{3,2,0,1:T(8,128)(2,1)S(1)} %get-tuple-element.20), kind=kOutput, calls=%fused_computation.19 | convolution fusion | flops 1062720000 | bytes 8340480 | tf_op jit(solution)/shard_map/rjch,rjcd->jhd/dot_general | solution.py:71
  374.9 8.4 %copy.91 = bf16[2,180,2880]{1,0,2:T(2,128)(2,1)} copy(bf16[2,180,2880]{2,1,0:T(8,128)(2,1)} %fusion.25) | data formatting | bytes 4147200
  383.4 7.4 %reshape.70 = bf16[2880,360]{1,0:T(8,128)(2,1)} reshape(bf16[2880,2,180]{2,1,0:T(2,128)(2,1)} %bitcast.61) | data formatting | bytes 4147200
  390.8 5.6 %fusion.28 = bf16[2,180,2880]{2,1,0:T(8,128)(2,1)} fusion(bf16[64,2,8,2880]{3,2,1,0:T(8,128)(2,1)} %bitcast.64, bf16[64,2,8,180]{3,2,0,1:T(8,128)(2,1)S(1)} %get-tuple-element.19), kind=kOutput, calls=%fused_computation.20 | convolution fusion | flops 1062720000 | bytes 8340480 | tf_op jit(solution)/shard_map/rjch,rjcd->jhd/dot_general | solution.py:68
  396.5 8.4 %copy.89 = bf16[2,180,2880]{1,0,2:T(2,128)(2,1)} copy(bf16[2,180,2880]{2,1,0:T(8,128)(2,1)} %fusion.28) | data formatting | bytes 4147200
  404.9 7.6 %reshape.68 = bf16[2880,360]{1,0:T(8,128)(2,1)} reshape(bf16[2880,2,180]{2,1,0:T(2,128)(2,1)} %bitcast.62) | data formatting | bytes 4147200
  412.5 3.7 all-to-all-start.2
  416.2 26.4 %reduce-scatter.17.cloned.1.call-done = bf16[720,360]{1,0:T(8,128)(2,1)} async-done(((bf16[2880,360]{1,0:T(8,128)(2,1)}), bf16[720,360]{1,0:T(8,128)(2,1)}) %reduce-scatter.17.cloned.1.call-update) | async-done | bytes 518416
  442.7 2.5 reshape.73
  445.2 2.5 copy.70
  447.7 30.6 %reduce-scatter.15.cloned.1.call-done = bf16[720,360]{1,0:T(8,128)(2,1)} async-done(((bf16[2880,360]{1,0:T(8,128)(2,1)}), bf16[720,360]{1,0:T(8,128)(2,1)}) %reduce-scatter.15.cloned.1.call-update) | async-done | bytes 518416
  478.3 2.5 reshape.71
  480.9 2.5 copy.69
  483.4 30.4 %reduce-scatter.13.cloned.1.call-done = bf16[720,360]{1,0:T(8,128)(2,1)} async-done(((bf16[2880,360]{1,0:T(8,128)(2,1)}), bf16[720,360]{1,0:T(8,128)(2,1)}) %reduce-scatter.13.cloned.1.call-update) | async-done | bytes 518416
  513.8 2.5 reshape.69
  516.4 2.5 copy.68
  518.9 0.8 convolution_convert_fusion.2
  (17 shorter events, 0.2 us)
Async XLA Ops:
  7.2 324.7 %copy-start = (bf16[2,180,2880]{2,0,1:T(2,128)(2,1)S(1)}, bf16[2,180,2880]{2,0,1:T(2,128)(2,1)}, u32[]{:S(2)}) copy-start(bf16[2,180,2880]{2,0,1:T(2,128)(2,1)} %param.12) | copy-start | bytes 6220804
  7.2 405.3 %reduce-scatter.11.cloned.1.call-start = ((), (), s32[]{:S(2)}) async-start(), calls=%async_computation.7 | async-start | bytes 6406144 | tf_op jit(solution)/shard_map/reduce_scatter | solution.py:82
  324.3 5.3 %copy-start.2 = (bf16[1,16,1,4,16,2880]{5,4,3,1,2,0:T(8,128)(2,1)S(1)}, bf16[1,16,1,4,16,2880]{5,4,3,1,2,0:T(8,128)(2,1)}, u32[]{:S(2)}) copy-start(bf16[1,16,1,4,16,2880]{5,4,3,1,2,0:T(8,128)(2,1)} %get-tuple-element.17) | copy-start | bytes 17694724
  324.3 5.7 %copy-start.3 = (bf16[2,180,2880]{2,0,1:T(2,128)(2,1)S(1)}, bf16[2,180,2880]{2,0,1:T(2,128)(2,1)}, u32[]{:S(2)}) copy-start(bf16[2,180,2880]{2,0,1:T(2,128)(2,1)} %param.11) | copy-start | bytes 6220804
  346.8 1.0 copy-start.4
  346.8 95.9 %reduce-scatter.17.cloned.1.call-start = ((), (), s32[]{:S(2)}) async-start(), calls=%async_computation.10 | async-start | bytes 2764800
  369.3 109.0 %reduce-scatter.15.cloned.1.call-start = ((), (), s32[]{:S(2)}) async-start(), calls=%async_computation.9 | async-start | bytes 2764800
  390.8 123.0 %reduce-scatter.13.cloned.1.call-start = ((), (), s32[]{:S(2)}) async-start(), calls=%async_computation.8 | async-start | bytes 2764800
  404.9 114.8 %copy-start.1 = (bf16[2,180,2880]{2,0,1:T(2,128)(2,1)S(1)}, bf16[2,180,2880]{2,0,1:T(2,128)(2,1)}, u32[]{:S(2)}) copy-start(bf16[2,180,2880]{2,0,1:T(2,128)(2,1)} %param.12) | copy-start | bytes 6220804
  412.5 106.4 %all-to-all-start.2 = ((bf16[4,16,2880]{2,1,0:T(8,128)(2,1)}), bf16[4,16,2880]{2,1,0:T(8,128)(2,1)S(1)}, u32[]{:S(2)}, u32[]{:S(2)}) async-start(bf16[4,16,2880]{2,1,0:T(8,128)(2,1)} %bitcast.77), calls=%async_computation.3 | async-start | bytes 753664 | tf_op jit(solution)/shard_map/all_to_all | solution.py:89
Sparse Core Ops, SparseCore 0:
  346.9 58.3 reduce-scatter.10
  407.9 34.7 reduce-scatter.16
  445.3 33.0 reduce-scatter.14
  480.8 33.0 reduce-scatter.12
